TPU v7x, 256 devices: a whole 4x4x8 slice. The times are simulated.
256 devices in a mesh: seq: 32 (over x, z), tp: 8 (over y, core).
Axes of the slice: x: 4, y: 4, z: 8, core: 2. Of those that a mesh axis runs over, the one named last changes fastest.
Arguments:
- event_vectors: bfloat16 [16384, 6144], P('seq'), may hold values from -6 to 6
- question_projector: bfloat16 [6144, 4096], P('seq', 'tp'), may hold values from -0.078125 to 0.078125
- lookup_projector: bfloat16 [6144, 4096], P('seq', 'tp'), may hold values from -0.078125 to 0.078125
- content_projector: bfloat16 [6144, 4096], P('seq', 'tp'), may hold values from -0.078125 to 0.078125
- channel_fading_speed: float32 [32], P('tp'), may hold values from 1.2207031e-05 to 0.03334
- surge_fading: float32 [16384], P('seq'), may hold values from -0.6932 to 0, as said below
- channel_scaling_coefficient: float32 [4096], P('tp'), may hold values from 0.1 to 1.9
- final_projector: bfloat16 [4096, 6144], P('seq', 'tp'), may hold values from -0.09375 to 0.09375
Outputs:
- mixed: bfloat16 [16384, 6144], P('seq', 'tp')
Inputs may be any that keep to these rules, and one draw needn't show every extreme that they name: `surge_fading`: zero at all but a few positions of the sequence.
All inputs are finite; a program needn't handle non-finite values.
Results may differ from a plain program's by a relative error of at most 0.0063.
Values may be sent and summed in bfloat16 or wider, within the bound.
A program may use at most 128 MiB of HBM per device.

v0:
```python
import jax
import jax.numpy as jnp
from jax import lax
from jax.sharding import PartitionSpec as P

HD = 128
SPAN_LENGTH = 512


def entering(part, axis, combine, identity):
    place = lax.axis_index(axis)
    gathered = jax.tree.map(lambda a: lax.all_gather(a, axis), part)
    state = jax.tree.map(lambda a, e: jnp.zeros_like(a) + jnp.asarray(e, a.dtype), part, identity)

    def one(step, state):
        return combine(
            state, jax.tree.map(lambda a: lax.dynamic_index_in_dim(a, step, 0, False), gathered)
        )

    return lax.fori_loop(0, place, one, state)


def block_pass(carry, inputs):
    carried, before = carry
    query_block, key_block, value_block, log_block = inputs
    inside = jnp.cumsum(log_block, axis=0)
    block_total = inside[-1]
    highest = lax.Precision.HIGHEST
    scores = jnp.einsum("thd,shd->hts", query_block, key_block, precision=highest)
    spread_log = inside.T[:, :, None] - inside.T[:, None, :]
    rows_index = lax.broadcasted_iota(jnp.int32, (SPAN_LENGTH, SPAN_LENGTH), 0)
    cols_index = lax.broadcasted_iota(jnp.int32, (SPAN_LENGTH, SPAN_LENGTH), 1)
    causal = (rows_index >= cols_index)[None, :, :]
    weight = jnp.where(causal, jnp.exp(jnp.where(causal, spread_log, 0.0)), 0.0)
    within = jnp.einsum("hts,shd->thd", scores * weight, value_block, precision=highest)
    across = jnp.einsum(
        "thd,hde->the", query_block * jnp.exp(inside)[:, :, None], carried, precision=highest
    )
    updated = jnp.exp(block_total)[:, None, None] * carried + jnp.einsum(
        "shd,she->hde",
        key_block * jnp.exp(block_total[None, :] - inside)[:, :, None],
        value_block,
        precision=highest,
    )
    factor = jnp.exp(before[None, :] + inside)
    return ((updated, before + block_total), (within + across, factor))


def chain_combine(earlier, later):
    return (earlier[0] + later[0], jnp.exp(later[0])[:, None, None] * earlier[1] + later[1])


def local(
    event_vectors,
    question_projector,
    lookup_projector,
    content_projector,
    channel_fading_speed,
    surge_fading,
    channel_scaling_coefficient,
    final_projector,
):
    tok_count = event_vectors.shape[0]
    number_of_heads = channel_fading_speed.shape[0]

    def project_rows(shard_rows):
        return jnp.dot(event_vectors, shard_rows, preferred_element_type=jnp.float32)

    query_sum = project_rows(lax.all_gather(question_projector, "seq", axis=0, tiled=True))
    key_sum = project_rows(lax.all_gather(lookup_projector, "seq", axis=0, tiled=True))
    value_sum = project_rows(lax.all_gather(content_projector, "seq", axis=0, tiled=True))
    queries = jax.nn.silu(query_sum).astype(jnp.bfloat16)
    keys_act = jax.nn.silu(key_sum).astype(jnp.bfloat16)
    values_act = value_sum.astype(jnp.bfloat16)
    span_count = tok_count // SPAN_LENGTH
    shaped = (span_count, SPAN_LENGTH, number_of_heads, HD)
    query_blocks = queries.astype(jnp.float32).reshape(shaped)
    key_blocks = keys_act.astype(jnp.float32).reshape(shaped)
    value_blocks = values_act.astype(jnp.float32).reshape(shaped)
    stepwise_fading_exponent = (surge_fading[:, None] - channel_fading_speed[None, :]).reshape(
        (span_count, SPAN_LENGTH, number_of_heads)
    )
    start = (
        jnp.zeros((number_of_heads, HD, HD), jnp.float32),
        jnp.zeros((number_of_heads,), jnp.float32),
    )
    (local_state, local_log), (outputs, factors) = lax.scan(
        block_pass, start, (query_blocks, key_blocks, value_blocks, stepwise_fading_exponent)
    )
    identity = (
        jnp.zeros((number_of_heads,), jnp.float32),
        jnp.zeros((number_of_heads, HD, HD), jnp.float32),
    )
    prior_log, incoming = entering((local_log, local_state), "seq", chain_combine, identity)
    query_flat = query_blocks.reshape((tok_count, number_of_heads, HD))
    reached = jnp.einsum("thd,hde->the", query_flat, incoming, precision=lax.Precision.HIGHEST)
    attention = (
        outputs.reshape((tok_count, number_of_heads, HD))
        + factors.reshape((tok_count, number_of_heads))[:, :, None] * reached
    )
    meansq = jnp.mean(attention * attention, axis=-1, keepdims=True)
    normed = (
        attention
        / jnp.sqrt(meansq + 1e-05)
        * channel_scaling_coefficient.reshape((number_of_heads, HD))[None, :, :]
    )
    normed = normed.reshape((tok_count, number_of_heads * HD)).astype(jnp.bfloat16)
    every_head = lax.all_gather(normed, "tp", axis=1, tiled=True)
    mixed = jnp.dot(
        every_head,
        lax.all_gather(final_projector, "seq", axis=0, tiled=True),
        preferred_element_type=jnp.float32,
    )
    return mixed.astype(jnp.bfloat16)


def solution(mesh):
    in_specs = (
        P("seq", None),
        P("seq", "tp"),
        P("seq", "tp"),
        P("seq", "tp"),
        P("tp"),
        P("seq"),
        P("tp"),
        P("seq", "tp"),
    )
    out_specs = P("seq", "tp")
    return jax.shard_map(local, mesh=mesh, in_specs=in_specs, out_specs=out_specs, check_vma=False)
```

profile of v0, /device:TPU:1, one launch (start us, length us, event | category | flops | bytes accessed | tf_op | source)
XLA Modules:
  0.0 514.1 jit_solution(17631043664003188020)
XLA Ops:
  6.5 0.7 all-gather.9.cloned.1.call-update
  7.3 0.7 all-gather.13.cloned.1.call-update
  8.1 0.7 all-gather.11.cloned.1.call-update
  8.8 0.8 broadcast_subtract_fusion
  9.6 1.2 reduce-window.6
  11.5 90.6 %all-gather.9.cloned.1.call-done = bf16[6144,512]{1,0:T(8,128)(2,1)} async-done(((bf16[192,512]{1,0:T(8,128)(2,1)}), bf16[6144,512]{1,0:T(8,128)(2,1)}) %all-gather.9.cloned.1.call-update) | async-done | bytes 6291472 | tf_op jit(solution)/shard_map/all_gather | solution.py:71
  102.1 8.1 %convolution_convert_fusion.1 = bf16[512,512]{0,1:T(8,128)(2,1)S(1)} fusion(bf16[512,6144]{1,0:T(8,128)(2,1)} %param.10, bf16[6144,512]{1,0:T(8,128)(2,1)} %all-gather.9.cloned.1.call-done), kind=kOutput, calls=%fused_computation.18 | convolution fusion | flops 3221487616 | bytes 13107200 | tf_op jit(solution)/shard_map/dot_general | solution.py:67
  110.2 80.2 %all-gather.13.cloned.1.call-done = bf16[6144,512]{1,0:T(8,128)(2,1)} async-done(((bf16[192,512]{1,0:T(8,128)(2,1)}), bf16[6144,512]{1,0:T(8,128)(2,1)}) %all-gather.13.cloned.1.call-update) | async-done | bytes 6291472 | tf_op jit(solution)/shard_map/all_gather | solution.py:70
  190.4 8.2 %multiply_convert_fusion.1 = bf16[512,512]{0,1:T(8,128)(2,1)S(1)} fusion(bf16[512,6144]{1,0:T(8,128)(2,1)} %param.10, bf16[6144,512]{1,0:T(8,128)(2,1)} %all-gather.13.cloned.1.call-done), kind=kOutput, calls=%fused_computation.27 | convolution fusion | flops 3222536192 | bytes 13107200 | tf_op jit(solution)/shard_map/dot_general | solution.py:67
  198.6 1.4 convolution_add_fusion.1
  200.0 0.5 all-gather.17.cloned.1.call-update
  200.6 31.6 %all-gather.1 = f32[32,1,4]{2,1,0:T(1,128)S(1)} all-gather(f32[1,1,4]{2,1,0:T(1,128)S(1)} %bitcast.69), channel_id=1, replica_groups=mesh['seq'=32,'tp'=8] {'seq'}, dimensions={0}, use_global_device_ids=true | all-gather | bytes 528 | tf_op jit(solution)/shard_map/all_gather | solution.py:12
  232.3 46.4 %all-gather.11.cloned.1.call-done = bf16[6144,512]{1,0:T(8,128)(2,1)} async-done(((bf16[192,512]{1,0:T(8,128)(2,1)}), bf16[6144,512]{1,0:T(8,128)(2,1)}) %all-gather.11.cloned.1.call-update) | async-done | bytes 6291472 | tf_op jit(solution)/shard_map/all_gather | solution.py:69
  278.7 8.2 %multiply_convert_fusion.2 = bf16[512,512]{0,1:T(8,128)(2,1)S(1)} fusion(bf16[512,6144]{1,0:T(8,128)(2,1)} %param.10, bf16[6144,512]{1,0:T(8,128)(2,1)} %all-gather.11.cloned.1.call-done), kind=kOutput, calls=%fused_computation.28 | convolution fusion | flops 3222536192 | bytes 13107200 | tf_op jit(solution)/shard_map/dot_general | solution.py:67
  286.9 0.7 fusion.23
  287.6 3.7 fusion
  291.3 1.0 fusion.12
  292.4 84.0 %all-gather.19.cloned.1.call-done = f32[128,128,128]{2,1,0:T(8,128)} async-done(((f32[4,128,128]{2,1,0:T(8,128)}), f32[128,128,128]{2,1,0:T(8,128)}) %all-gather.19.cloned.1.call-update) | async-done | bytes 8388624 | tf_op jit(solution)/shard_map/all_gather | solution.py:12
  376.4 0.2 while.3
  376.6 0.7 multiply_reduce_fusion
  377.4 0.9 multiply_convert_fusion
  378.4 86.3 %all-gather.17.cloned.1.call-done = bf16[4096,768]{1,0:T(8,128)(2,1)} async-done(((bf16[128,768]{1,0:T(8,128)(2,1)}), bf16[4096,768]{1,0:T(8,128)(2,1)}) %all-gather.17.cloned.1.call-update) | async-done | bytes 6291472 | tf_op jit(solution)/shard_map/all_gather | solution.py:111
  464.6 34.2 %all-gather.15.cloned.1.call-done = bf16[512,4096]{0,1:T(8,128)(2,1)} async-done(((bf16[512,512]{0,1:T(8,128)(2,1)}), bf16[512,4096]{0,1:T(8,128)(2,1)}) %all-gather.15.cloned.1.call-update) | async-done | bytes 4194320 | tf_op jit(solution)/shard_map/all_gather | solution.py:108
  498.8 8.4 %convolution_convert_fusion = bf16[512,768]{1,0:T(8,128)(2,1)} fusion(bf16[512,4096]{0,1:T(8,128)(2,1)} %all-gather.15.cloned.1.call-done, bf16[4096,768]{1,0:T(8,128)(2,1)} %all-gather.17.cloned.1.call-done), kind=kOutput, calls=%fused_computation.12 | convolution fusion | flops 3221618688 | bytes 11272192 | tf_op jit(solution)/shard_map/dot_general | solution.py:109
  (20 shorter events, 1.0 us)
Async XLA Ops:
  6.5 95.6 %all-gather.9.cloned.1.call-start = ((), (), s32[]{:S(2)}) async-start(), calls=%async_computation | async-start | bytes 6488064 | tf_op jit(solution)/shard_map/all_gather | solution.py:71
  7.3 183.1 %all-gather.13.cloned.1.call-start = ((), (), s32[]{:S(2)}) async-start(), calls=%async_computation.2 | async-start | bytes 6488064 | tf_op jit(solution)/shard_map/all_gather | solution.py:70
  8.0 270.7 %all-gather.11.cloned.1.call-start = ((), (), s32[]{:S(2)}) async-start(), calls=%async_computation.1 | async-start | bytes 6488064 | tf_op jit(solution)/shard_map/all_gather | solution.py:69
  8.7 367.6 %all-gather.19.cloned.1.call-start = ((), (), s32[]{:S(2)}) async-start(), calls=%async_computation.5 | async-start | bytes 8650752 | tf_op jit(solution)/shard_map/all_gather | solution.py:12
  200.0 264.7 %all-gather.17.cloned.1.call-start = ((), (), s32[]{:S(2)}) async-start(), calls=%async_computation.4 | async-start | bytes 6488064 | tf_op jit(solution)/shard_map/all_gather | solution.py:111
  200.6 298.3 %all-gather.15.cloned.1.call-start = ((), (), s32[]{:S(2)}) async-start(), calls=%async_computation.3 | async-start | bytes 4718592 | tf_op jit(solution)/shard_map/all_gather | solution.py:108
  291.3 86.1 %copy-start = (f32[512]{0:T(512)S(1)}, f32[512]{0:T(512)}, u32[]{:S(2)}) copy-start(f32[512]{0:T(512)} %param.16) | copy-start | bytes 6148
Sparse Core Ops, SparseCore 0:
  9.9 92.1 all-gather.8
  104.7 85.6 all-gather.12
  192.9 85.6 all-gather.10
  281.1 95.1 all-gather.18
  378.8 85.8 all-gather.16
  466.3 32.4 all-gather.14
where the time goes:
time: 515 us; the launch traced here: 514 us
  waiting for transfers between devices  424 us (82%)
  matrix products  40.4 us (8%)
  blocking collectives  31.6 us (6%)
  between operations  13.6 us (3%)
    all_gather x1, waiting for transfers between devices, local(): lax.all_gather(content_projector, 'seq', axis=0, tiled=True)  90.6 us
    all_gather x1, waiting for transfers between devices, local(): lax.all_gather(final_projector, 'seq', axis=0, tiled=True)  86.3 us
    all_gather x1, waiting for transfers between devices, entering(): gathered = jax.tree.map(lambda a: lax.all_gather(a, axis), part)  84 us
    all_gather x1, waiting for transfers between devices, local(): lax.all_gather(lookup_projector, 'seq', axis=0, tiled=True)  80.2 us
    all_gather x1, waiting for transfers between devices, local(): lax.all_gather(question_projector, 'seq', axis=0, tiled=True)  46.4 us
    all_gather x1, waiting for transfers between devices, local(): every_head = lax.all_gather(normed, 'tp', axis=1, tiled=True)  34.2 us
    all_gather x1, blocking collectives, entering(): gathered = jax.tree.map(lambda a: lax.all_gather(a, axis), part)  31.6 us
    dot_general x3, matrix products, project_rows(): jnp.dot(event_vectors, shard_rows, preferred_element_type=jnp.float32)  24.4 us
  transfers between devices with their start and end apart: 6, of which 6 were waited for; matrix products, arithmetic and copies ran while one was open for 7% of the time, Pallas kernels for 0%

commit v1 on v0

--- a/solution.py
+++ b/solution.py
@@ -5,6 +5,34 @@
 
 HD = 128
 SPAN_LENGTH = 512
+
+
+def start_the_matrix(incoming_x, mesh_dim, pos_dim):
+    w2, passed, oldest = (
+        lax.axis_size(mesh_dim),
+        lax.axis_index(mesh_dim),
+        incoming_x.shape[pos_dim],
+    )
+    seen = [(h, (h + 1) % w2) for h in range(w2)]
+    mat_out = jnp.zeros(
+        (*incoming_x.shape[:pos_dim], w2 * oldest, *incoming_x.shape[pos_dim + 1 :]),
+        incoming_x.dtype,
+    )
+    history = [(h, (h - 1) % w2) for h in range(w2)]
+    mat_out = lax.dynamic_update_slice_in_dim(mat_out, incoming_x, passed * oldest, axis=pos_dim)
+    tmp = w2 // 2
+    outcome_arr = latest = incoming_x
+    for dd in range(1, tmp + 1):
+        outcome_arr = lax.ppermute(outcome_arr, axis_name=mesh_dim, perm=seen)
+        mat_out = lax.dynamic_update_slice_in_dim(
+            mat_out, outcome_arr, (passed - dd) % w2 * oldest, axis=pos_dim
+        )
+        if dd < w2 - tmp:
+            latest = lax.ppermute(latest, axis_name=mesh_dim, perm=history)
+            mat_out = lax.dynamic_update_slice_in_dim(
+                mat_out, latest, (passed + dd) % w2 * oldest, axis=pos_dim
+            )
+    return mat_out
 
 
 def entering(part, axis, combine, identity):
@@ -105,7 +133,7 @@
         * channel_scaling_coefficient.reshape((number_of_heads, HD))[None, :, :]
     )
     normed = normed.reshape((tok_count, number_of_heads * HD)).astype(jnp.bfloat16)
-    every_head = lax.all_gather(normed, "tp", axis=1, tiled=True)
+    every_head = start_the_matrix(normed, "tp", pos_dim=1)
     mixed = jnp.dot(
         every_head,
         lax.all_gather(final_projector, "seq", axis=0, tiled=True),

time: 515 us -> 481 us (0.934)
  waiting for transfers between devices: 424 us -> 371 us
  starting transfers between devices: 0.2 us -> 11.3 us
  local copies, waits for them, and re-layouts: 0.37 us -> 9.27 us
    all_gather x1 -> x0, waiting for transfers between devices: 34.2 us -> none  [local(): every_head = lax.all_gather(normed, 'tp', axis=1, tiled=True)]
    all_gather x1, waiting for transfers between devices: 86.3 us -> 52.1 us  [local(): lax.all_gather(final_projector, 'seq', axis=0, tiled=True)]
    ppermute x0 -> x7, waiting for transfers between devices: none -> 15 us  [the longest x4 14.9 us: start_the_matrix(): outcome_arr = lax.ppermute(outcome_arr, axis_name=mesh_dim, perm=seen)]
    ppermute x0 -> x7, starting transfers between devices: none -> 11.1 us  [the longest x4 9.63 us: start_the_matrix(): outcome_arr = lax.ppermute(outcome_arr, axis_name=mesh_dim, perm=seen)]
    dynamic_update_slice x0 -> x8, local copies, waits for them, and re-layouts: none -> 6.66 us  [the longest x4 3.34 us: start_the_matrix(): lax.dynamic_update_slice_in_dim(mat_out, outcome_arr, (passed - dd) % w2...]
  transfers between devices with their start and end apart: 6 -> 12, of which waited for: 6 -> 10; matrix products, arithmetic and copies ran while one was open for 7% -> 9% of each run, Pallas kernels for 0% -> 0%
where the time goes in v1:
time: 481 us; the launch traced here: 480 us
  waiting for transfers between devices  371 us (77%)
  matrix products  40.4 us (8%)
  blocking collectives  31.6 us (7%)
  between operations  13.3 us (3%)
  starting transfers between devices  11.3 us (2%)
  local copies, waits for them, and re-layouts  9.27 us (2%)
    all_gather x1, waiting for transfers between devices, local(): lax.all_gather(content_projector, 'seq', axis=0, tiled=True)  90.6 us
    all_gather x1, waiting for transfers between devices, entering(): gathered = jax.tree.map(lambda a: lax.all_gather(a, axis), part)  84 us
    all_gather x1, waiting for transfers between devices, local(): lax.all_gather(lookup_projector, 'seq', axis=0, tiled=True)  80.2 us
    all_gather x1, waiting for transfers between devices, local(): lax.all_gather(final_projector, 'seq', axis=0, tiled=True)  52.1 us
    all_gather x1, waiting for transfers between devices, local(): lax.all_gather(question_projector, 'seq', axis=0, tiled=True)  46.4 us
    all_gather x1, blocking collectives, entering(): gathered = jax.tree.map(lambda a: lax.all_gather(a, axis), part)  31.6 us
    dot_general x3, matrix products, project_rows(): jnp.dot(event_vectors, shard_rows, preferred_element_type=jnp.float32)  24.4 us
    ppermute x4, waiting for transfers between devices, start_the_matrix(): outcome_arr = lax.ppermute(outcome_arr, axis_name=mesh_dim, perm=seen)  14.9 us
  transfers between devices with their start and end apart: 12, of which 10 were waited for; matrix products, arithmetic and copies ran while one was open for 9% of the time, Pallas kernels for 0%

profile of v1, /device:TPU:1, one launch (start us, length us, event | category | flops | bytes accessed | tf_op | source)
XLA Modules:
  0.0 479.6 jit_solution(6585737655859538075)
XLA Ops:
  9.6 1.2 reduce-window.6
  11.5 90.6 %all-gather.8.cloned.1.call-done = bf16[6144,512]{1,0:T(8,128)(2,1)} async-done(((bf16[192,512]{1,0:T(8,128)(2,1)}), bf16[6144,512]{1,0:T(8,128)(2,1)}) %all-gather.8.cloned.1.call-update) | async-done | bytes 6291472 | tf_op jit(solution)/shard_map/all_gather | solution.py:99
  102.1 8.1 %convolution_convert_fusion.1 = bf16[512,512]{0,1:T(8,128)(2,1)S(1)} fusion(bf16[512,6144]{1,0:T(8,128)(2,1)} %param.10, bf16[6144,512]{1,0:T(8,128)(2,1)} %all-gather.8.cloned.1.call-done), kind=kOutput, calls=%fused_computation.18 | convolution fusion | flops 3221487616 | bytes 13107200 | tf_op jit(solution)/shard_map/dot_general | solution.py:95
  110.2 80.2 %all-gather.12.cloned.1.call-done = bf16[6144,512]{1,0:T(8,128)(2,1)} async-done(((bf16[192,512]{1,0:T(8,128)(2,1)}), bf16[6144,512]{1,0:T(8,128)(2,1)}) %all-gather.12.cloned.1.call-update) | async-done | bytes 6291472 | tf_op jit(solution)/shard_map/all_gather | solution.py:98
  190.4 8.2 %multiply_convert_fusion.1 = bf16[512,512]{0,1:T(8,128)(2,1)S(1)} fusion(bf16[512,6144]{1,0:T(8,128)(2,1)} %param.10, bf16[6144,512]{1,0:T(8,128)(2,1)} %all-gather.12.cloned.1.call-done), kind=kOutput, calls=%fused_computation.27 | convolution fusion | flops 3222536192 | bytes 13107200 | tf_op jit(solution)/shard_map/dot_general | solution.py:95
  198.6 1.4 convolution_add_fusion.1
  200.6 31.6 %all-gather.1 = f32[32,1,4]{2,1,0:T(1,128)S(1)} all-gather(f32[1,1,4]{2,1,0:T(1,128)S(1)} %bitcast.71), channel_id=1, replica_groups=mesh['seq'=32,'tp'=8] {'seq'}, dimensions={0}, use_global_device_ids=true | all-gather | bytes 528 | tf_op jit(solution)/shard_map/all_gather | solution.py:40
  232.3 46.4 %all-gather.10.cloned.1.call-done = bf16[6144,512]{1,0:T(8,128)(2,1)} async-done(((bf16[192,512]{1,0:T(8,128)(2,1)}), bf16[6144,512]{1,0:T(8,128)(2,1)}) %all-gather.10.cloned.1.call-update) | async-done | bytes 6291472 | tf_op jit(solution)/shard_map/all_gather | solution.py:97
  278.7 8.2 %multiply_convert_fusion.2 = bf16[512,512]{0,1:T(8,128)(2,1)S(1)} fusion(bf16[512,6144]{1,0:T(8,128)(2,1)} %param.10, bf16[6144,512]{1,0:T(8,128)(2,1)} %all-gather.10.cloned.1.call-done), kind=kOutput, calls=%fused_computation.28 | convolution fusion | flops 3222536192 | bytes 13107200 | tf_op jit(solution)/shard_map/dot_general | solution.py:95
  287.6 3.7 fusion
  291.3 1.0 fusion.12
  292.4 84.0 %all-gather.16.cloned.1.call-done = f32[128,128,128]{2,1,0:T(8,128)} async-done(((f32[4,128,128]{2,1,0:T(8,128)}), f32[128,128,128]{2,1,0:T(8,128)}) %all-gather.16.cloned.1.call-update) | async-done | bytes 8388624 | tf_op jit(solution)/shard_map/all_gather | solution.py:40
  377.5 2.2 collective-permute-start
  379.7 6.1 %collective-permute-done = bf16[512,512]{0,1:T(8,128)(2,1)S(1)} collective-permute-done((bf16[512,512]{0,1:T(8,128)(2,1)S(1)}, bf16[512,512]{0,1:T(8,128)(2,1)S(1)}, u32[]{:S(2)}, u32[]{:S(2)}) %collective-permute-start) | collective-permute-done | bytes 524320 | tf_op jit(solution)/shard_map/ppermute | solution.py:26
  385.9 2.5 collective-permute-start.2
  388.5 6.0 %collective-permute-done.2 = bf16[512,512]{0,1:T(8,128)(2,1)S(1)} collective-permute-done((bf16[512,512]{0,1:T(8,128)(2,1)S(1)}, bf16[512,512]{0,1:T(8,128)(2,1)S(1)}, u32[]{:S(2)}, u32[]{:S(2)}) %collective-permute-start.2) | collective-permute-done | bytes 524320 | tf_op jit(solution)/shard_map/ppermute | solution.py:26
  394.5 2.5 collective-permute-start.4
  396.9 2.2 broadcast_in_dim.52
  400.0 1.3 collective-permute-start.5
  402.2 0.9 collective-permute-done.4
  403.1 2.5 collective-permute-start.6
  409.8 1.9 collective-permute-done.6
  412.5 52.1 %all-gather.14.cloned.1.call-done = bf16[4096,768]{1,0:T(8,128)(2,1)} async-done(((bf16[128,768]{1,0:T(8,128)(2,1)}), bf16[4096,768]{1,0:T(8,128)(2,1)}) %all-gather.14.cloned.1.call-update) | async-done | bytes 6291472 | tf_op jit(solution)/shard_map/all_gather | solution.py:139
  464.6 8.4 %convolution_convert_fusion = bf16[512,768]{1,0:T(8,128)(2,1)} fusion(bf16[512,4096]{0,1:T(8,128)(2,1)} %constant_dynamic-update-slice_fusion, bf16[4096,768]{1,0:T(8,128)(2,1)} %all-gather.14.cloned.1.call-done), kind=kOutput, calls=%fused_computation.12 | convolution fusion | flops 3221618688 | bytes 11272192 | tf_op jit(solution)/shard_map/dot_general | solution.py:137
  (40 shorter events, 13.1 us)
Async XLA Ops:
  6.5 95.6 %all-gather.8.cloned.1.call-start = ((), (), s32[]{:S(2)}) async-start(), calls=%async_computation | async-start | bytes 6488064 | tf_op jit(solution)/shard_map/all_gather | solution.py:99
  7.3 183.1 %all-gather.12.cloned.1.call-start = ((), (), s32[]{:S(2)}) async-start(), calls=%async_computation.2 | async-start | bytes 6488064 | tf_op jit(solution)/shard_map/all_gather | solution.py:98
  8.0 270.7 %all-gather.10.cloned.1.call-start = ((), (), s32[]{:S(2)}) async-start(), calls=%async_computation.1 | async-start | bytes 6488064 | tf_op jit(solution)/shard_map/all_gather | solution.py:97
  8.7 367.6 %all-gather.16.cloned.1.call-start = ((), (), s32[]{:S(2)}) async-start(), calls=%async_computation.4 | async-start | bytes 8650752 | tf_op jit(solution)/shard_map/all_gather | solution.py:40
  200.0 264.7 %all-gather.14.cloned.1.call-start = ((), (), s32[]{:S(2)}) async-start(), calls=%async_computation.3 | async-start | bytes 6488064 | tf_op jit(solution)/shard_map/all_gather | solution.py:139
  292.4 85.0 %copy-start = (f32[512]{0:T(512)S(1)}, f32[512]{0:T(512)}, u32[]{:S(2)}) copy-start(f32[512]{0:T(512)} %param.16) | copy-start | bytes 6148
  377.5 8.3 %collective-permute-start = (bf16[512,512]{0,1:T(8,128)(2,1)S(1)}, bf16[512,512]{0,1:T(8,128)(2,1)S(1)}, u32[]{:S(2)}, u32[]{:S(2)}) collective-permute-start(bf16[512,512]{0,1:T(8,128)(2,1)S(1)} %bitcast.61), channel_id=1, source_target_pairs={{0,1},{1,2},{2,3},{3,4},{4,5},{5,6},{6,7},{7,0},{8,9},{9,10},{10,1... | collective-permute-start | bytes 1572872 | tf_op jit(solution)/shard_map/ppermute | solution.py:26
  379.7 8.6 %collective-permute-start.1 = (bf16[512,512]{0,1:T(8,128)(2,1)S(1)}, bf16[512,512]{0,1:T(8,128)(2,1)S(1)}, u32[]{:S(2)}, u32[]{:S(2)}) collective-permute-start(bf16[512,512]{0,1:T(8,128)(2,1)S(1)} %bitcast.62), channel_id=1, source_target_pairs={{0,7},{1,0},{2,1},{3,2},{4,3},{5,4},{6,5},{7,6},{8,15},{9,8},{10,9... | collective-permute-start | bytes 1572872 | tf_op jit(solution)/shard_map/ppermute | solution.py:31
  385.9 8.6 %collective-permute-start.2 = (bf16[512,512]{0,1:T(8,128)(2,1)S(1)}, bf16[512,512]{0,1:T(8,128)(2,1)S(1)}, u32[]{:S(2)}, u32[]{:S(2)}) collective-permute-start(bf16[512,512]{0,1:T(8,128)(2,1)S(1)} %collective-permute-done), channel_id=1, source_target_pairs={{0,1},{1,2},{2,3},{3,4},{4,5},{5,6},{6,7},{7,0},{8,9},{9,10},{10,1... | collective-permute-start | bytes 1572872 | tf_op jit(solution)/shard_map/ppermute | solution.py:26
  388.3 11.7 %collective-permute-start.3 = (bf16[512,512]{0,1:T(8,128)(2,1)S(1)}, bf16[512,512]{0,1:T(8,128)(2,1)S(1)}, u32[]{:S(2)}, u32[]{:S(2)}) collective-permute-start(bf16[512,512]{0,1:T(8,128)(2,1)S(1)} %collective-permute-done.1), channel_id=1, source_target_pairs={{0,7},{1,0},{2,1},{3,2},{4,3},{5,4},{6,5},{7,6},{8,15},{9,8},{10,9... | collective-permute-start | bytes 1572872 | tf_op jit(solution)/shard_map/ppermute | solution.py:31
  394.5 8.6 %collective-permute-start.4 = (bf16[512,512]{0,1:T(8,128)(2,1)S(1)}, bf16[512,512]{0,1:T(8,128)(2,1)S(1)}, u32[]{:S(2)}, u32[]{:S(2)}) collective-permute-start(bf16[512,512]{0,1:T(8,128)(2,1)S(1)} %collective-permute-done.2), channel_id=1, source_target_pairs={{0,1},{1,2},{2,3},{3,4},{4,5},{5,6},{6,7},{7,0},{8,9},{9,10},{10,1... | collective-permute-start | bytes 1572872 | tf_op jit(solution)/shard_map/ppermute | solution.py:26
  400.0 9.0 %collective-permute-start.5 = (bf16[512,512]{0,1:T(8,128)(2,1)S(1)}, bf16[512,512]{0,1:T(8,128)(2,1)S(1)}, u32[]{:S(2)}, u32[]{:S(2)}) collective-permute-start(bf16[512,512]{0,1:T(8,128)(2,1)S(1)} %collective-permute-done.3), channel_id=1, source_target_pairs={{0,7},{1,0},{2,1},{3,2},{4,3},{5,4},{6,5},{7,6},{8,15},{9,8},{10,9... | collective-permute-start | bytes 1572872 | tf_op jit(solution)/shard_map/ppermute | solution.py:31
  403.1 8.6 %collective-permute-start.6 = (bf16[512,512]{0,1:T(8,128)(2,1)S(1)}, bf16[512,512]{0,1:T(8,128)(2,1)S(1)}, u32[]{:S(2)}, u32[]{:S(2)}) collective-permute-start(bf16[512,512]{0,1:T(8,128)(2,1)S(1)} %collective-permute-done.4), channel_id=1, source_target_pairs={{0,1},{1,2},{2,3},{3,4},{4,5},{5,6},{6,7},{7,0},{8,9},{9,10},{10,1... | collective-permute-start | bytes 1572872 | tf_op jit(solution)/shard_map/ppermute | solution.py:26
Sparse Core Ops, SparseCore 0:
  9.9 92.1 all-gather.7
  104.7 85.6 all-gather.11
  192.9 85.6 all-gather.9
  281.1 95.1 all-gather.15
  378.8 85.8 all-gather.13
